TPU v7x, 32 devices: a whole 2x2x4 slice. The times are simulated.
32 devices in a mesh: tm: 8 (over y, x, core), head: 4 (over z).
Axes of the slice: x: 2, y: 2, z: 4, core: 2. Of those that a mesh axis runs over, the one named last changes fastest.
Arguments:
- inputs: bfloat16 [32768, 1024], P(('tm', 'head')), may hold values from -54 to 54
- weights: bfloat16 [1024, 768], P(('tm', 'head')), may hold values from -0.1875 to 0.1875
- band_lists: int32 [256, 5], P('tm'), may hold values from 0 to 1, as said below
Outputs:
- attended: bfloat16 [32768, 256], P(('tm', 'head'))
Inputs may be any that keep to these rules, and one draw needn't show every extreme that they name: band_lists[b, 2] is 1 for every block b.
All inputs are finite; a program needn't handle non-finite values.
Results may differ from a plain program's by a relative error of at most 0.0045.
The roundings to bfloat16 on the way count: a program that leaves them out, or rounds other values in their place, can miss the bound.
Values may be sent and summed in bfloat16 or wider, within the bound.
A program may use at most 64 MiB of HBM per device.

v0:
```python
import functools

import jax
import jax.numpy as jnp
from jax import lax
from jax.experimental import pallas as pl
from jax.experimental.pallas import tpu as pltpu
from jax.sharding import PartitionSpec as P

HD = 64
BLK = 128
REACH = 2
SPAN = 2 * REACH + 1
MARGIN = REACH * BLK
GROUP = 2
MESH = pl.DeviceIdType.MESH


def attend_block(b, g, first, row0, total_blocks, band_ref, q_buf, kv_buf, out_ref):
    lanes = GROUP * HD
    start = pl.multiple_of(b * BLK, BLK)
    rows = pl.ds(start, BLK)
    window = pl.ds(start, SPAN * BLK)
    bias = []
    for o in range(SPAN):
        key_block = first + b + o - REACH
        ok = (band_ref[o, row0 + b] == 1) & (key_block >= 0) & (key_block < total_blocks)
        bias.append(jnp.where(ok, 0.0, -jnp.inf).astype(jnp.float32))
    head_of = lax.broadcasted_iota(jnp.int32, (BLK, lanes), 1) // HD
    here = slice(g * lanes, (g + 1) * lanes)
    q = q_buf[rows, here]
    k = kv_buf[g, window, :lanes]
    v = kv_buf[g, window, lanes:]
    stacked = jnp.concatenate(
        [jnp.where(head_of == h, q, jnp.zeros_like(q)) for h in range(GROUP)], axis=0
    )
    s = lax.dot_general(stacked, k, (((1,), (1,)), ((), ())), preferred_element_type=jnp.float32)
    parts = [s[:, o * BLK : (o + 1) * BLK] + bias[o] for o in range(SPAN)]
    m = jnp.max(functools.reduce(jnp.maximum, parts), axis=1, keepdims=True)
    probs = [jnp.exp(part - m) for part in parts]
    total = jnp.sum(functools.reduce(jnp.add, probs), axis=1, keepdims=True)
    p = jnp.concatenate([x.astype(jnp.bfloat16) for x in probs], axis=1)
    mixed = jnp.dot(p, v, preferred_element_type=jnp.float32)
    num, den = mixed[:BLK], jnp.broadcast_to(total[:BLK], (BLK, lanes))
    for h in range(1, GROUP):
        part = slice(h * BLK, (h + 1) * BLK)
        num = jnp.where(head_of == h, mixed[part], num)
        den = jnp.where(head_of == h, jnp.broadcast_to(total[part], (BLK, lanes)), den)
    out_ref[rows, here] = (num / den).astype(out_ref.dtype)


def kernel(
    tms, nheads, x_hbm, w_hbm, band_hbm, out_ref,
    x_buf, w_ref, w_buf, kv_buf, q_buf, band_ref,
    x_sem, band_sem, w_sem, w_send, w_recv, halo_send, halo_recv,
):
    tm, hd = lax.axis_index("tm"), lax.axis_index("head")
    shard = w_ref.shape[0]
    rows = x_buf.shape[0]
    heads = w_ref.shape[1] // (3 * HD)
    blocks = rows // BLK
    count = tms * nheads

    def owner(t, h):
        return t * nheads + h

    def z_peer(d):
        return lax.rem(hd + d, nheads)

    me = owner(tm, hd)
    nxt, prv = lax.rem(me + 1, count), lax.rem(me + count - 1, count)
    nxt_id = (nxt // nheads, lax.rem(nxt, nheads))
    prv_id = (prv // nheads, lax.rem(prv, nheads))

    def flip(t, bit):
        return t + bit - 2 * bit * lax.rem(t // bit, 2)

    sib, side, front = flip(tm, 1), flip(tm, 2), flip(tm, 4)
    diag = flip(side, 4)

    barrier = pltpu.get_barrier_semaphore()
    for d in range(1, nheads):
        pl.semaphore_signal(barrier, inc=1, device_id=(tm, z_peer(d)), device_id_type=MESH)
    for t in (side, front, diag, sib):
        pl.semaphore_signal(barrier, inc=1, device_id=(t, hd), device_id_type=MESH)

    w_copy = pltpu.make_async_copy(w_hbm, w_ref, w_sem)
    w_copy.start()
    x_copy = pltpu.make_async_copy(x_hbm, x_buf, x_sem)
    x_copy.start()
    band_copy = pltpu.make_async_copy(band_hbm, band_ref, band_sem)
    band_copy.start()

    w_copy.wait()
    w = w_ref[...].astype(jnp.float32)
    groups = heads // GROUP

    def columns(part, hs):
        return [w[:, (3 * h + part) * HD : (3 * h + part + 1) * HD] for h in hs]

    own = pl.ds(pl.multiple_of(me * shard, shard), shard)
    for g in range(groups):
        hs = range(g * GROUP, (g + 1) * GROUP)
        w_buf[g, own, :] = jnp.concatenate(columns(1, hs) + columns(2, hs), axis=1).astype(
            jnp.bfloat16
        )
    w_buf[groups, own, :] = jnp.concatenate(columns(0, range(heads)), axis=1).astype(jnp.bfloat16)
    pl.semaphore_wait(barrier, nheads - 1 + 4)

    sent = [[], [], []]
    direct = (0,)

    def slot(kind, t, h):
        return w_buf.at[kind, pl.ds(pl.multiple_of(owner(t, h) * shard, shard), shard)]

    def send(kind, t, h, device):
        copy = pltpu.make_async_remote_copy(
            src_ref=slot(kind, t, h), dst_ref=slot(kind, t, h),
            send_sem=w_send.at[kind, len(sent[kind])], recv_sem=w_recv.at[kind, owner(t, h)],
            device_id=device, device_id_type=MESH,
        )
        copy.start()
        sent[kind].append(copy)

    def arrived(kind, t, h):
        pltpu.make_async_remote_copy(
            src_ref=slot(kind, t, h), dst_ref=slot(kind, t, h),
            send_sem=x_sem, recv_sem=w_recv.at[kind, owner(t, h)],
            device_id=(sib, hd), device_id_type=MESH,
        ).wait_recv()

    def to_z(kind):
        for d in range(1, nheads):
            send(kind, tm, hd, (tm, z_peer(d)))

    def spread(kind, d):
        for t in (diag, side, front, sib) if kind in direct else (side, front, sib):
            send(kind, tm, z_peer(d), (t, hd))

    def from_z(kind):
        for d in range(1, nheads):
            arrived(kind, tm, z_peer(d))
            spread(kind, d)

    def from_plane(kind):
        for d in range(nheads):
            h = z_peer(d)
            for t, relay, onward in ((side, 0, front), (front, 1, side)):
                arrived(kind, t, h)
                if kind not in direct and d % 2 == relay:
                    send(kind, t, h, (onward, hd))
                send(kind, t, h, (sib, hd))

    def from_diag(kind):
        for d in range(nheads):
            arrived(kind, diag, z_peer(d))
            send(kind, diag, z_peer(d), (sib, hd))

    def from_sib(kind):
        for t in (tm, side, front, diag):
            for d in range(nheads):
                arrived(kind, flip(t, 1), z_peer(d))

    def project_kv(g, start, size):
        kv_buf[g, MARGIN + start : MARGIN + start + size, :] = jnp.dot(
            x_buf[start : start + size, :], w_buf[g], preferred_element_type=jnp.float32
        ).astype(jnp.bfloat16)

    def halo(g, far, up):
        if up:
            src, dst = (rows, 0) if far else (rows + BLK, BLK)
        else:
            src = MARGIN + BLK if far else MARGIN
            dst = src + rows
        at = 2 * far + up
        return pltpu.make_async_remote_copy(
            src_ref=kv_buf.at[g, pl.ds(src, BLK)], dst_ref=kv_buf.at[g, pl.ds(dst, BLK)],
            send_sem=halo_send.at[g, at], recv_sem=halo_recv.at[g, at],
            device_id=nxt_id if up else prv_id, device_id_type=MESH,
        )

    halos = [[[halo(g, far, up) for up in (0, 1)] for far in (0, 1)] for g in range(groups)]

    def trade(g):
        project_kv(g, 0, MARGIN)
        project_kv(g, rows - MARGIN, MARGIN)
        project_kv(g, MARGIN, BLK)
        (near_down, near_up), (far_down, far_up) = halos[g]

        @pl.when(hd == nheads - 1)
        def _():
            for copy in (near_up, far_up, near_down, far_down):
                copy.start()

        @pl.when(hd == 0)
        def _():
            for copy in (near_down, far_down, near_up, far_up):
                copy.start()

        @pl.when((hd > 0) & (hd < nheads - 1))
        def _():
            for copy in (near_down, near_up, far_down, far_up):
                copy.start()

    to_z(0)
    spread(0, 0)
    to_z(1)
    from_z(0)
    to_z(2)
    from_plane(0)
    spread(1, 0)
    from_z(1)
    from_diag(0)
    x_copy.wait()
    from_sib(0)
    trade(0)
    from_plane(1)
    spread(2, 0)
    from_z(2)
    from_diag(1)
    from_sib(1)
    trade(1)
    from_plane(2)
    from_diag(2)
    for g in range(groups):
        project_kv(g, MARGIN + BLK, rows - 2 * MARGIN - BLK)
    from_sib(2)
    for start in range(0, rows, MARGIN):
        q = jnp.dot(
            x_buf[start : start + MARGIN, :], w_buf[groups], preferred_element_type=jnp.float32
        ).astype(jnp.bfloat16)
        q_buf[start : start + MARGIN, :] = q * jnp.bfloat16(HD ** -0.5)
    band_copy.wait()

    args = (me * blocks, hd * blocks, count * blocks, band_ref, q_buf, kv_buf, out_ref)

    @pl.loop(REACH, blocks - REACH)
    def _(b):
        for g in range(groups):
            attend_block(b, g, *args)

    for g in range(groups):
        for far in (0, 1):
            for copy in halos[g][far]:
                copy.wait()
            for b in ((0, blocks - 1) if far else (1, blocks - 2)):
                attend_block(b, g, *args)

    for copy in sent[0] + sent[1] + sent[2]:
        copy.wait_send()


def fused(tms, nheads, inputs, weights, band_lists):
    rows, depth = inputs.shape
    columns = weights.shape[1]
    width = columns // 3
    count = tms * nheads
    sends = nheads - 1 + 3 * nheads + 3 * nheads + nheads
    dma = pltpu.SemaphoreType.DMA
    return pl.pallas_call(
        functools.partial(kernel, tms, nheads),
        out_shape=jax.ShapeDtypeStruct((rows, width), jnp.bfloat16),
        in_specs=[
            pl.BlockSpec(memory_space=pl.ANY),
            pl.BlockSpec(memory_space=pl.ANY),
            pl.BlockSpec(memory_space=pl.ANY),
        ],
        out_specs=pl.BlockSpec(memory_space=pltpu.VMEM),
        scratch_shapes=[
            pltpu.VMEM((rows, depth), jnp.bfloat16),
            pltpu.VMEM(weights.shape, jnp.bfloat16),
            pltpu.VMEM((3, depth, width), jnp.bfloat16),
            pltpu.VMEM((2, rows + 2 * MARGIN, width), jnp.bfloat16),
            pltpu.VMEM((rows, width), jnp.bfloat16),
            pltpu.SMEM(band_lists.shape[::-1], jnp.int32),
            dma,
            dma,
            dma,
            dma((3, sends)),
            dma((3, count)),
            dma((2, 4)),
            dma((2, 4)),
        ],
        compiler_params=pltpu.CompilerParams(collective_id=0, has_side_effects=True),
    )(inputs, weights, band_lists.T)


def padded(block, width):
    count = lax.axis_size("tm")
    forward = [(i, i + 1) for i in range(count - 1)]
    backward = [(target, source) for source, target in forward]
    low = lax.ppermute(block[block.shape[0] - width :], "tm", forward)
    high = lax.ppermute(block[:width], "tm", backward)
    return jnp.concatenate([low, block, high], axis=0)


def attend_masked(query, keys, values, valid):
    blocks = query.shape[0] // BLK
    key_blocks = keys.reshape(blocks + 2 * REACH, BLK, HD)
    value_blocks = values.reshape(blocks + 2 * REACH, BLK, HD)
    banded_keys = jnp.stack([key_blocks[o : o + blocks] for o in range(SPAN)], axis=1)
    banded_values = jnp.stack([value_blocks[o : o + blocks] for o in range(SPAN)], axis=1)
    scores = jnp.einsum(
        "nxf,nmzf->nxmz", query.reshape(blocks, BLK, HD), banded_keys,
        preferred_element_type=jnp.float32,
    ) * HD ** (-0.5)
    scores = jnp.where(valid[:, None, :, None], scores, -jnp.inf)
    probs = jnp.exp(scores - jnp.max(scores, axis=(2, 3), keepdims=True))
    total = jnp.sum(probs, axis=(2, 3))
    mixed = jnp.einsum(
        "afuv,auvl->afl", probs.astype(jnp.bfloat16), banded_values,
        preferred_element_type=jnp.float32,
    )
    return (mixed / total[:, :, None]).reshape(blocks * BLK, HD)


def by_head(inputs, weights, band_lists):
    inputs = lax.all_gather(inputs, "head", axis=0, tiled=True)
    rows = inputs.shape[0]
    head_cols = lax.all_to_all(weights, "head", split_axis=1, concat_axis=0, tiled=True)
    projected = jnp.dot(
        inputs, lax.all_gather(head_cols, "tm", axis=0, tiled=True),
        preferred_element_type=jnp.float32,
    ).astype(jnp.bfloat16)
    blocks = rows // BLK
    query_block = lax.axis_index("tm") * blocks + jnp.arange(blocks, dtype=jnp.int32)
    key_block = query_block[:, None] + jnp.arange(SPAN, dtype=jnp.int32)[None, :] - REACH
    valid = (band_lists == 1) & (key_block >= 0) & (key_block < blocks * lax.axis_size("tm"))
    outs = []
    for h in range(head_cols.shape[1] // (3 * HD)):
        q, k, v = (
            projected[:, (3 * h + part) * HD : (3 * h + part + 1) * HD] for part in range(3)
        )
        keyvals = padded(jnp.concatenate([k, v], axis=1), MARGIN)
        outs.append(attend_masked(q, keyvals[:, :HD], keyvals[:, HD:], valid))
    out = jnp.concatenate(outs, axis=1).astype(jnp.bfloat16)
    return lax.all_to_all(out, "head", split_axis=0, concat_axis=1, tiled=True)


def solution(mesh):
    tms, nheads = mesh.shape["tm"], mesh.shape["head"]

    def on_device(inputs, weights, band_lists):
        heads = weights.shape[1] // (3 * HD)
        small = weights.shape[0] % 16 or inputs.shape[0] < 2 * MARGIN + BLK
        if small or heads != 2 * GROUP or inputs.shape[0] % MARGIN or tms != 8:
            return by_head(inputs, weights, band_lists)
        return fused(tms, nheads, inputs, weights, band_lists)

    return jax.shard_map(
        on_device,
        mesh=mesh,
        in_specs=(P(("tm", "head"), None), P(("tm", "head"), None), P("tm", None)),
        out_specs=P(("tm", "head"), None),
        check_vma=False,
    )
```

profile of v0, /device:TPU:0, one launch (start us, length us, event | category | flops | bytes accessed | tf_op | source)
XLA Modules:
  0.0 36.8 jit_solution(3290792831100723369)
XLA Ops:
  0.0 34.9 %shard_map.37 = bf16[1024,256]{1,0:T(8,128)(2,1)} custom-call(bf16[1024,1024]{1,0:T(8,128)(2,1)} %x_hbm.1, bf16[32,768]{1,0:T(8,128)(2,1)} %w_hbm.1, s32[5,32]{1,0:T(8,128)} %bitcast.1), custom_call_target="tpu_custom_call" | custom-call | tf_op jit(solution)/shard_map/pallas_call | solution.py:260
  34.9 1.9 %copy.5 = bf16[1024,256]{1,0:T(8,128)(2,1)} copy(bf16[1024,256]{1,0:T(8,128)(2,1)} %shard_map.37) | data formatting | bytes 1048576
where the time goes:
time: 37 us; the launch traced here: 36.8 us
  Pallas kernels  34.9 us (94%)
  local copies, waits for them, and re-layouts  1.87 us (5%)
    pallas_call x1, Pallas kernels, fused(): pl.pallas_call(functools.partial(kernel, tms, nheads), out_shape=jax.Shap...  34.9 us
    unnamed x1, local copies, waits for them, and re-layouts  1.87 us

commit v1 on v0

--- a/solution.py
+++ b/solution.py
@@ -281,8 +281,8 @@
             dma((2, 4)),
             dma((2, 4)),
         ],
-        compiler_params=pltpu.CompilerParams(collective_id=0, has_side_effects=True),
-    )(inputs, weights, band_lists.T)
+        compiler_params=pltpu.CompilerParams(collective_id=0, has_side_effects=True, vmem_limit_bytes=16*1024*1024),
+    )(*(pltpu.with_memory_space_constraint(a, pltpu.HBM) for a in (inputs, weights, band_lists.T)))
 
 
 def padded(block, width):

time: 37 us -> 35.1 us (0.949)
  local copies, waits for them, and re-layouts: 1.87 us -> 0.8 us
  Pallas kernels: 34.9 us -> 34.1 us
    unnamed x1, local copies, waits for them, and re-layouts: 1.87 us -> 0.8 us
    pallas_call x1, Pallas kernels: 34.9 us -> 34.1 us  [fused(): pl.pallas_call(functools.partial(kernel, tms, nheads), out_shape=jax.Shap...]
where the time goes in v1:
time: 35.1 us; the launch traced here: 35 us
  Pallas kernels  34.1 us (97%)
  local copies, waits for them, and re-layouts  0.8 us (2%)
    pallas_call x1, Pallas kernels, fused(): pl.pallas_call(functools.partial(kernel, tms, nheads), out_shape=jax.Shap...  34.1 us
    unnamed x1, local copies, waits for them, and re-layouts  0.8 us

profile of v1, /device:TPU:0, one launch (start us, length us, event | category | flops | bytes accessed | tf_op | source)
XLA Modules:
  0.0 35.0 jit_solution(379184789914419748)
XLA Ops:
  0.0 34.1 %shard_map.37 = bf16[1024,256]{1,0:T(8,128)(2,1)S(1)} custom-call(bf16[1024,1024]{1,0:T(8,128)(2,1)} %x_hbm.1, bf16[32,768]{1,0:T(8,128)(2,1)} %w_hbm.1, s32[5,32]{1,0:T(8,128)} %bitcast.1), custom_call_target="tpu_custom_call" | custom-call | tf_op jit(solution)/shard_map/pallas_call | solution.py:260
  34.2 0.8 %copy.5 = bf16[1024,256]{1,0:T(8,128)(2,1)} copy(bf16[1024,256]{1,0:T(8,128)(2,1)S(1)} %shard_map.37) | data formatting | bytes 1048576

commit v2 on v1

--- a/solution.py
+++ b/solution.py
@@ -108,7 +108,7 @@
     pl.semaphore_wait(barrier, nheads - 1 + 4)
 
     sent = [[], [], []]
-    direct = (0,)
+    direct = (0, 1)
 
     def slot(kind, t, h):
         return w_buf.at[kind, pl.ds(pl.multiple_of(owner(t, h) * shard, shard), shard)]
@@ -184,7 +184,6 @@
     def trade(g):
         project_kv(g, 0, MARGIN)
         project_kv(g, rows - MARGIN, MARGIN)
-        project_kv(g, MARGIN, BLK)
         (near_down, near_up), (far_down, far_up) = halos[g]
 
         @pl.when(hd == nheads - 1)
@@ -202,28 +201,24 @@
             for copy in (near_down, near_up, far_down, far_up):
                 copy.start()
 
-    to_z(0)
-    spread(0, 0)
-    to_z(1)
-    from_z(0)
-    to_z(2)
+    for kind in range(3):
+        to_z(kind)
+        spread(kind, 0)
+    for kind in range(3):
+        from_z(kind)
     from_plane(0)
-    spread(1, 0)
-    from_z(1)
     from_diag(0)
     x_copy.wait()
     from_sib(0)
     trade(0)
     from_plane(1)
-    spread(2, 0)
-    from_z(2)
     from_diag(1)
     from_sib(1)
     trade(1)
     from_plane(2)
     from_diag(2)
     for g in range(groups):
-        project_kv(g, MARGIN + BLK, rows - 2 * MARGIN - BLK)
+        project_kv(g, MARGIN, rows - 2 * MARGIN)
     from_sib(2)
     for start in range(0, rows, MARGIN):
         q = jnp.dot(

time: 35.1 us -> 31.6 us (0.900)
  Pallas kernels: 34.1 us -> 30.7 us
    pallas_call x1, Pallas kernels: 34.1 us -> 30.7 us  [fused(): pl.pallas_call(functools.partial(kernel, tms, nheads), out_shape=jax.Shap...]
where the time goes in v2:
time: 31.6 us; the launch traced here: 31.5 us
  Pallas kernels  30.7 us (97%)
  local copies, waits for them, and re-layouts  0.8 us (3%)
    pallas_call x1, Pallas kernels, fused(): pl.pallas_call(functools.partial(kernel, tms, nheads), out_shape=jax.Shap...  30.7 us
    unnamed x1, local copies, waits for them, and re-layouts  0.8 us

profile of v2, /device:TPU:0, one launch (start us, length us, event | category | flops | bytes accessed | tf_op | source)
XLA Modules:
  0.0 31.5 jit_solution(1932748966850381970)
XLA Ops:
  0.0 30.7 %shard_map.37 = bf16[1024,256]{1,0:T(8,128)(2,1)S(1)} custom-call(bf16[1024,1024]{1,0:T(8,128)(2,1)} %x_hbm.1, bf16[32,768]{1,0:T(8,128)(2,1)} %w_hbm.1, s32[5,32]{1,0:T(8,128)} %bitcast.1), custom_call_target="tpu_custom_call" | custom-call | tf_op jit(solution)/shard_map/pallas_call | solution.py:255
  30.7 0.8 %copy.5 = bf16[1024,256]{1,0:T(8,128)(2,1)} copy(bf16[1024,256]{1,0:T(8,128)(2,1)S(1)} %shard_map.37) | data formatting | bytes 1048576

commit v3 on v2

--- a/solution.py
+++ b/solution.py
@@ -52,7 +52,7 @@
 def kernel(
     tms, nheads, x_hbm, w_hbm, band_hbm, out_ref,
     x_buf, w_ref, w_buf, kv_buf, q_buf, band_ref,
-    x_sem, band_sem, w_sem, w_send, w_recv, halo_send, halo_recv,
+    x_edge, x_sem, band_sem, w_sem, edge_send, edge_recv, w_send, w_recv, halo_send, halo_recv,
 ):
     tm, hd = lax.axis_index("tm"), lax.axis_index("head")
     shard = w_ref.shape[0]
@@ -179,6 +179,22 @@
             device_id=nxt_id if up else prv_id, device_id_type=MESH,
         )
 
+    odd, end = lax.rem(tm, 2), hd // (nheads - 1)
+    turn_up = (odd == 0) & (hd == nheads - 1)
+    turn_down = (odd == 1) & (hd == 0)
+    edge_copy = pltpu.make_async_remote_copy(
+        src_ref=x_buf.at[pl.ds(pl.multiple_of(BLK + end * (rows - MARGIN - BLK), BLK), BLK)],
+        dst_ref=x_edge, send_sem=edge_send, recv_sem=edge_recv,
+        device_id=(sib, nheads - 1 - hd), device_id_type=MESH,
+    )
+
+    def project_edge():
+        at = pl.multiple_of(end * (MARGIN + BLK + rows), BLK)
+        for g in range(groups):
+            kv_buf[g, pl.ds(at, BLK), :] = jnp.dot(
+                x_edge[...], w_buf[g], preferred_element_type=jnp.float32
+            ).astype(jnp.bfloat16)
+
     halos = [[[halo(g, far, up) for up in (0, 1)] for far in (0, 1)] for g in range(groups)]
 
     def trade(g):
@@ -186,36 +202,44 @@
         project_kv(g, rows - MARGIN, MARGIN)
         (near_down, near_up), (far_down, far_up) = halos[g]
 
+        def begin(*copies):
+            for copy in copies:
+                copy.start()
+
         @pl.when(hd == nheads - 1)
         def _():
-            for copy in (near_up, far_up, near_down, far_down):
-                copy.start()
+            begin(near_up)
+            pl.when(odd == 1)(far_up.start)
+            begin(near_down, far_down)
 
         @pl.when(hd == 0)
         def _():
-            for copy in (near_down, far_down, near_up, far_up):
-                copy.start()
+            begin(near_down)
+            pl.when(odd == 0)(far_down.start)
+            begin(near_up, far_up)
 
         @pl.when((hd > 0) & (hd < nheads - 1))
         def _():
-            for copy in (near_down, near_up, far_down, far_up):
-                copy.start()
+            begin(near_down, near_up, far_down, far_up)
 
     for kind in range(3):
         to_z(kind)
         spread(kind, 0)
-    for kind in range(3):
+    from_z(0)
+    x_copy.wait()
+    for kind in range(1, 3):
         from_z(kind)
+    pl.when(turn_up | turn_down)(edge_copy.start)
     from_plane(0)
     from_diag(0)
-    x_copy.wait()
     from_sib(0)
     trade(0)
     from_plane(1)
     from_diag(1)
+    from_plane(2)
     from_sib(1)
     trade(1)
-    from_plane(2)
+
     from_diag(2)
     for g in range(groups):
         project_kv(g, MARGIN, rows - 2 * MARGIN)
@@ -234,13 +258,30 @@
         for g in range(groups):
             attend_block(b, g, *args)
 
+    @pl.when(turn_up | turn_down)
+    def _():
+        edge_copy.wait_recv()
+        project_edge()
+
     for g in range(groups):
         for far in (0, 1):
-            for copy in halos[g][far]:
-                copy.wait()
+            down, up = halos[g][far]
+            if far:
+                pl.when(jnp.logical_not(turn_up))(down.wait_recv)
+                pl.when(jnp.logical_not(turn_down))(up.wait_recv)
+            else:
+                down.wait_recv()
+                up.wait_recv()
             for b in ((0, blocks - 1) if far else (1, blocks - 2)):
                 attend_block(b, g, *args)
 
+    for g in range(groups):
+        (near_down, near_up), (far_down, far_up) = halos[g]
+        near_down.wait_send()
+        near_up.wait_send()
+        pl.when(jnp.logical_not(turn_down))(far_down.wait_send)
+        pl.when(jnp.logical_not(turn_up))(far_up.wait_send)
+    pl.when(turn_up | turn_down)(edge_copy.wait_send)
     for copy in sent[0] + sent[1] + sent[2]:
         copy.wait_send()
 
@@ -268,6 +309,9 @@
             pltpu.VMEM((2, rows + 2 * MARGIN, width), jnp.bfloat16),
             pltpu.VMEM((rows, width), jnp.bfloat16),
             pltpu.SMEM(band_lists.shape[::-1], jnp.int32),
+            pltpu.VMEM((BLK, depth), jnp.bfloat16),
+            dma,
+            dma,
             dma,
             dma,
             dma,
@@ -338,7 +382,7 @@
     def on_device(inputs, weights, band_lists):
         heads = weights.shape[1] // (3 * HD)
         small = weights.shape[0] % 16 or inputs.shape[0] < 2 * MARGIN + BLK
-        if small or heads != 2 * GROUP or inputs.shape[0] % MARGIN or tms != 8:
+        if small or heads != 2 * GROUP or inputs.shape[0] % MARGIN or tms != 8 or nheads < 2:
             return by_head(inputs, weights, band_lists)
         return fused(tms, nheads, inputs, weights, band_lists)
 

time: 31.6 us -> 31.4 us (level)
  no operation moved by 1% of the time
where the time goes in v3:
time: 31.4 us; the launch traced here: 31.2 us
  Pallas kernels  30.4 us (97%)
  local copies, waits for them, and re-layouts  0.8 us (3%)
    pallas_call x1, Pallas kernels, fused(): pl.pallas_call(functools.partial(kernel, tms, nheads), out_shape=jax.Shap...  30.4 us
    unnamed x1, local copies, waits for them, and re-layouts  0.8 us

profile of v3, /device:TPU:0, one launch (start us, length us, event | category | flops | bytes accessed | tf_op | source)
XLA Modules:
  0.0 31.2 jit_solution(15709823141889446486)
XLA Ops:
  0.0 30.4 %shard_map.37 = bf16[1024,256]{1,0:T(8,128)(2,1)S(1)} custom-call(bf16[1024,1024]{1,0:T(8,128)(2,1)} %x_hbm.1, bf16[32,768]{1,0:T(8,128)(2,1)} %w_hbm.1, s32[5,32]{1,0:T(8,128)} %bitcast.1), custom_call_target="tpu_custom_call" | custom-call | tf_op jit(solution)/shard_map/pallas_call | solution.py:296
  30.5 0.8 %copy.5 = bf16[1024,256]{1,0:T(8,128)(2,1)} copy(bf16[1024,256]{1,0:T(8,128)(2,1)S(1)} %shard_map.37) | data formatting | bytes 1048576
